TPU v7x, 32 devices: a whole 2x2x4 slice. The times are simulated.
32 devices in a mesh: cluster: 16 (over z, y, x), ens: 2 (over core).
Axes of the slice: x: 2, y: 2, z: 4, core: 2. Of those that a mesh axis runs over, the one named last changes fastest.
Arguments:
- log_rate: float32 [16, 16384], P('ens', 'cluster'), may hold values from -1 to 0.5
- state: float32 [16, 16384], P('ens', 'cluster'), may hold values from -1 to 1
- rate_coef: float32 [16, 16384], P('ens', 'cluster'), may hold values from 0.5 to 2
- state_coef: float32 [16, 16384], P('ens', 'cluster'), may hold values from 0.5 to 2
- near_weight: bfloat16 [3, 16384, 1024], P(None, 'cluster', 'ens'), may hold values from -0.21582031 to 0.21582031
- col_basis: bfloat16 [64, 16384], P(None, 'cluster'), may hold values from -0.1875 to 0.1875
- coupling: float32 [1024, 1024], P('cluster'), may hold values from -0.1875 to 0.1875
- cluster_row_factors: float32 [64, 16384], P(None, 'cluster'), may hold values from -2.25 to 2.25
- ranks: int32 [16], P('cluster'), may hold values from 16 to 64, as said below
Outputs:
- log_rate_next: float32 [16, 16384], P('ens', 'cluster')
- state_next: float32 [16, 16384], P('ens', 'cluster')
Inputs may be any that keep to these rules, and one draw needn't show every extreme that they name: `ranks`: each cluster's rank lies in 16 to 64; some cluster has rank 64.
All inputs are finite; a program needn't handle non-finite values.
Results may differ from a plain program's by a relative error of at most 0.0017.
Values may be sent and summed in bfloat16 or wider, within the bound.
A program may use at most 64 MiB of HBM per device.

v0:
```python
import jax
import jax.numpy as jnp
from jax import lax
from jax.sharding import PartitionSpec as P

step_length = 0.5
damping = 0.5


def with_halo(shard, sides, width):
    for axis, dim in sides:
        peers, length = (lax.axis_size(axis), shard.shape[dim])
        up = [(i, (i + 1) % peers) for i in range(peers - 1)]
        down = [(j, i) for i, j in up]
        last = lax.slice_in_dim(shard, length - width, length, axis=dim)
        initial = lax.slice_in_dim(shard, 0, width, axis=dim)
        before = lax.ppermute(last, axis, up)
        after = lax.ppermute(initial, axis, down)
        shard = jnp.concatenate([before, shard, after], axis=dim)
    return shard


def near_field(deficit, near_blocks):
    rows = deficit.shape[1]
    extended = with_halo(deficit, (("cluster", 1),), rows)
    total = jnp.zeros((deficit.shape[0], rows), jnp.float32)
    for k in range(3):
        columns = extended[:, k * rows : (k + 1) * rows]
        total = total + lax.dot_general(
            columns, near_blocks[k], (((1,), (1,)), ((), ())), preferred_element_type=jnp.float32
        )
    return total


def far_field(deficit, col_basis, masked, cluster_row_factors, own_rank):
    rank_index = jnp.arange(col_basis.shape[0], dtype=jnp.int32)
    coef = lax.dot_general(
        deficit, col_basis, (((1,), (1,)), ((), ())), preferred_element_type=jnp.float32
    )
    coef = jnp.where(rank_index[None, :] < own_rank, coef, 0.0)
    compressed_sum = lax.dot_general(
        lax.all_gather(coef, "cluster", axis=1, tiled=True),
        masked,
        (((1,), (1,)), ((), ())),
        precision=lax.Precision.HIGHEST,
        preferred_element_type=jnp.float32,
    )
    compressed_sum = jnp.where(rank_index[None, :] < own_rank, compressed_sum, 0.0)
    return jnp.dot(
        compressed_sum,
        cluster_row_factors,
        precision=lax.Precision.HIGHEST,
        preferred_element_type=jnp.float32,
    )


def local(
    log_rate,
    state,
    rate_coef,
    state_coef,
    near_weight,
    col_basis,
    coupling,
    cluster_row_factors,
    ranks,
):
    widest_rank = coupling.shape[0]
    column_cluster = jnp.arange(coupling.shape[1], dtype=jnp.int32) // widest_rank
    mine = lax.axis_index("cluster")
    masked = jnp.where((jnp.abs(column_cluster - mine) > 1)[None, :], coupling, 0.0)
    own_rank = ranks[0]
    near_blocks = lax.all_gather(near_weight, "ens", axis=2, tiled=True)

    def rates(current_logarithm, state_now):
        rate = jnp.exp(current_logarithm)
        deficit = (rate - 1.0).astype(jnp.bfloat16)
        stress_rate = near_field(deficit, near_blocks) + far_field(
            deficit, col_basis, masked, cluster_row_factors, own_rank
        )
        state_rate = jnp.exp(-state_now) - rate
        rate_rate = (stress_rate - state_coef * state_rate) / (rate_coef + damping * rate)
        return (rate_rate, state_rate)

    rate_one, state_one = rates(log_rate, state)
    rate_two, state_two = rates(log_rate + step_length * rate_one, state + step_length * state_one)
    log_rate_next = log_rate + 0.5 * step_length * (rate_one + rate_two)
    state_next = state + 0.5 * step_length * (state_one + state_two)
    return (log_rate_next, state_next)


def solution(mesh):
    in_specs = (
        P("ens", "cluster"),
        P("ens", "cluster"),
        P("ens", "cluster"),
        P("ens", "cluster"),
        P(None, "cluster", "ens"),
        P(None, "cluster"),
        P("cluster", None),
        P(None, "cluster"),
        P("cluster"),
    )
    out_specs = (P("ens", "cluster"), P("ens", "cluster"))
    return jax.shard_map(local, mesh=mesh, in_specs=in_specs, out_specs=out_specs, check_vma=False)
```

profile of v0, /device:TPU:0, one launch (start us, length us, event | category | flops | bytes accessed | tf_op | source)
XLA Modules:
  0.0 122.7 jit_solution(456674179303856980)
XLA Ops:
  7.2 0.0 copy-start
  7.2 0.0 copy-start.3
  7.2 0.0 copy-start.2
  7.2 0.0 copy-start.1
  7.2 0.0 copy-start.4
  7.2 0.0 copy-start.5
  7.2 0.0 copy-start.6
  7.2 0.0 all-gather.4.cloned.1.call-start
  7.3 0.7 all-gather.4.cloned.1.call-update
  8.0 0.8 fusion.27
  8.8 1.3 %collective-permute-start.1 = (bf16[8,1024]{1,0:T(8,128)(2,1)S(1)}, bf16[8,1024]{1,0:T(8,128)(2,1)S(1)}, u32[]{:S(2)}, u32[]{:S(2)}) collective-permute-start(bf16[8,1024]{1,0:T(8,128)(2,1)S(1)} %fusion.27), channel_id=1, source_target_pairs={{2,0},{4,2},{6,4},{8,6},{10,8},{12,10},{14,12},{16,14},{18,16},{20... | collective-permute-start | bytes 49160 | tf_op jit(solution)/shard_map/ppermute | solution.py:18
  10.1 5.5 %collective-permute-start = (bf16[8,1024]{1,0:T(8,128)(2,1)S(1)}, bf16[8,1024]{1,0:T(8,128)(2,1)S(1)}, u32[]{:S(2)}, u32[]{:S(2)}) collective-permute-start(bf16[8,1024]{1,0:T(8,128)(2,1)S(1)} %fusion.27), channel_id=1, source_target_pairs={{0,2},{2,4},{4,6},{6,8},{8,10},{10,12},{12,14},{14,16},{16,18},{18... | collective-permute-start | bytes 49160 | tf_op jit(solution)/shard_map/ppermute | solution.py:17
  16.2 1.0 fusion.20
  17.3 39.7 %all-gather = f32[16,64,8]{1,2,0:T(8,128)S(1)} all-gather(f32[1,64,8]{1,2,0:T(8,128)S(1)} %fusion.20), channel_id=1, replica_groups=mesh['cluster'=16,'ens'=2] {'cluster'}, dimensions={0}, use_global_device_ids=true | all-gather | bytes 34816 | tf_op jit(solution)/shard_map/all_gather | solution.py:42
  57.0 0.1 reshape.26
  57.1 1.2 convolution_select_fusion.2
  58.3 0.0 copy-done
  58.3 0.3 fusion.36
  58.6 0.0 all-gather.4.cloned.1.call-done
  58.6 2.2 %fusion.3 = f32[8,1024]{1,0:T(8,128)S(1)} fusion(bf16[8,1024]{1,0:T(8,128)(2,1)S(1)} %fusion.27, bf16[3,1024,1024]{2,1,0:T(8,128)(2,1)} %all-gather.4.cloned.1.call-done), kind=kOutput, calls=%fused_computation.6 | convolution fusion | flops 16777216 | bytes 2146304 | tf_op jit(solution)/shard_map/dot_general | solution.py:29
  60.8 0.0 collective-permute-done.1
  60.8 2.2 %fusion.5 = f32[8,1024]{1,0:T(8,128)S(1)} fusion(bf16[8,1024]{1,0:T(8,128)(2,1)S(1)} %collective-permute-done.1, bf16[3,1024,1024]{2,1,0:T(8,128)(2,1)} %all-gather.4.cloned.1.call-done), kind=kOutput, calls=%fused_computation.8 | convolution fusion | flops 16777216 | bytes 2146304 | tf_op jit(solution)/shard_map/dot_general | solution.py:29
  63.1 0.0 collective-permute-done
  63.1 0.0 copy-done.3
  63.1 0.0 copy-done.4
  63.1 0.0 copy-done.5
  63.1 0.0 copy-done.6
  63.1 2.9 %multiply_add_fusion = (f32[8,1024]{1,0:T(8,128)}, bf16[8,1024]{1,0:T(8,128)(2,1)S(1)}, f32[8,1024]{1,0:T(8,128)S(1)}) fusion(f32[8,1024]{1,0:T(8,128)S(1)} %copy-done.4, f32[8,1024]{1,0:T(8,128)S(1)} %copy-done.3, f32[8,1024]{1,0:T(8,128)S(1)} %copy-done.5, f32[8,1024]{1,0:T(8,128)S(1)} %copy-done.6, f32[8,1024]{1,0:T(8,128)S(1)} %fusion.36, ...), kind=kOutput, calls=%fused_computation.34 | convolution fusion | flops 16949248 | bytes 2424832 | tf_op jit(solution)/shard_map/dot_general | solution.py:29
  66.0 0.0 copy-done.2
  66.0 0.1 fusion.19
  66.2 1.3 %collective-permute-start.3 = (bf16[8,1024]{1,0:T(8,128)(2,1)S(1)}, bf16[8,1024]{1,0:T(8,128)(2,1)S(1)}, u32[]{:S(2)}, u32[]{:S(2)}) collective-permute-start(bf16[8,1024]{1,0:T(8,128)(2,1)S(1)} %get-tuple-element.3), channel_id=1, source_target_pairs={{2,0},{4,2},{6,4},{8,6},{10,8},{12,10},{14,12},{16,14},{18,16},{20... | collective-permute-start | bytes 49160 | tf_op jit(solution)/shard_map/ppermute | solution.py:18
  67.5 4.5 %collective-permute-start.2 = (bf16[8,1024]{1,0:T(8,128)(2,1)S(1)}, bf16[8,1024]{1,0:T(8,128)(2,1)S(1)}, u32[]{:S(2)}, u32[]{:S(2)}) collective-permute-start(bf16[8,1024]{1,0:T(8,128)(2,1)S(1)} %get-tuple-element.3), channel_id=1, source_target_pairs={{0,2},{2,4},{4,6},{6,8},{8,10},{10,12},{12,14},{14,16},{16,18},{18... | collective-permute-start | bytes 49160 | tf_op jit(solution)/shard_map/ppermute | solution.py:17
  72.0 35.8 %all-gather.1 = f32[16,64,8]{1,2,0:T(8,128)S(1)} all-gather(f32[1,64,8]{1,2,0:T(8,128)S(1)} %fusion.19), channel_id=1, replica_groups=mesh['cluster'=16,'ens'=2] {'cluster'}, dimensions={0}, use_global_device_ids=true | all-gather | bytes 34816 | tf_op jit(solution)/shard_map/all_gather | solution.py:42
  107.8 0.1 reshape.28
  107.9 0.0 copy-done.1
  107.9 0.3 convolution_select_fusion
  108.2 2.3 %fusion.2 = f32[8,1024]{1,0:T(8,128)S(1)} fusion(bf16[8,1024]{1,0:T(8,128)(2,1)S(1)} %get-tuple-element.3, bf16[3,1024,1024]{2,1,0:T(8,128)(2,1)} %all-gather.4.cloned.1.call-done), kind=kOutput, calls=%fused_computation.5 | convolution fusion | flops 16777216 | bytes 2146304 | tf_op jit(solution)/shard_map/dot_general | solution.py:29
  110.5 0.3 fusion.37
  110.7 0.0 collective-permute-done.3
  110.8 2.2 %fusion.4 = f32[8,1024]{1,0:T(8,128)S(1)} fusion(bf16[8,1024]{1,0:T(8,128)(2,1)S(1)} %collective-permute-done.3, bf16[3,1024,1024]{2,1,0:T(8,128)(2,1)} %all-gather.4.cloned.1.call-done), kind=kOutput, calls=%fused_computation.7 | convolution fusion | flops 16777216 | bytes 2146304 | tf_op jit(solution)/shard_map/dot_general | solution.py:29
  113.0 0.0 collective-permute-done.2
  113.0 2.9 %fusion.18 = f32[8,1024]{1,0:T(8,128)} fusion(f32[8,1024]{1,0:T(8,128)S(1)} %copy-done.3, f32[8,1024]{1,0:T(8,128)S(1)} %get-tuple-element.4, f32[8,1024]{1,0:T(8,128)S(1)} %fusion.37, f32[8,1024]{1,0:T(8,128)S(1)} %fusion.4, f32[8,1024]{1,0:T(8,128)S(1)} %fusion.2, bf16[8,1024]{1,0:T(8,128)(2,1)S(1)} %collective-permute-done.2, ...), kind=kOutput, calls=%fused_computation.21 | convolution fusion | flops 16932864 | bytes 2408448 | tf_op jit(solution)/shard_map/dot_general | solution.py:29
  (4 shorter events, 0.0 us)
Async XLA Ops:
  7.2 51.1 %copy-start = (f32[64,1024]{1,0:T(8,128)S(1)}, f32[64,1024]{1,0:T(8,128)}, u32[]{:S(2)}) copy-start(f32[64,1024]{1,0:T(8,128)} %param.16) | copy-start | bytes 786436
  7.2 55.9 %copy-start.3 = (f32[8,1024]{1,0:T(8,128)S(1)}, f32[8,1024]{1,0:T(8,128)}, u32[]{:S(2)}) copy-start(f32[8,1024]{1,0:T(8,128)} %param.9) | copy-start | bytes 98308
  7.2 58.8 %copy-start.2 = (bf16[64,1024]{1,0:T(8,128)(2,1)S(1)}, bf16[64,1024]{1,0:T(8,128)(2,1)}, u32[]{:S(2)}) copy-start(bf16[64,1024]{1,0:T(8,128)(2,1)} %param.14) | copy-start | bytes 393220
  7.2 100.7 %copy-start.1 = (f32[64,1024]{1,0:T(8,128)S(1)}, f32[64,1024]{1,0:T(8,128)}, u32[]{:S(2)}) copy-start(f32[64,1024]{1,0:T(8,128)} %param.15) | copy-start | bytes 786436
  7.2 55.9 %copy-start.4 = (f32[8,1024]{1,0:T(8,128)S(1)}, f32[8,1024]{1,0:T(8,128)}, u32[]{:S(2)}) copy-start(f32[8,1024]{1,0:T(8,128)} %param.10) | copy-start | bytes 98308
  7.2 55.9 %copy-start.5 = (f32[8,1024]{1,0:T(8,128)S(1)}, f32[8,1024]{1,0:T(8,128)}, u32[]{:S(2)}) copy-start(f32[8,1024]{1,0:T(8,128)} %param.11) | copy-start | bytes 98308
  7.2 55.9 %copy-start.6 = (f32[8,1024]{1,0:T(8,128)S(1)}, f32[8,1024]{1,0:T(8,128)}, u32[]{:S(2)}) copy-start(f32[8,1024]{1,0:T(8,128)} %param.12) | copy-start | bytes 98308
  7.2 51.4 %all-gather.4.cloned.1.call-start = ((), (), s32[]{:S(2)}) async-start(), calls=%async_computation | async-start | bytes 9437184 | tf_op jit(solution)/shard_map/all_gather | solution.py:73
  8.8 52.1 %collective-permute-start.1 = (bf16[8,1024]{1,0:T(8,128)(2,1)S(1)}, bf16[8,1024]{1,0:T(8,128)(2,1)S(1)}, u32[]{:S(2)}, u32[]{:S(2)}) collective-permute-start(bf16[8,1024]{1,0:T(8,128)(2,1)S(1)} %fusion.27), channel_id=1, source_target_pairs={{2,0},{4,2},{6,4},{8,6},{10,8},{12,10},{14,12},{16,14},{18,16},{20... | collective-permute-start | bytes 49160 | tf_op jit(solution)/shard_map/ppermute | solution.py:18
  10.1 53.0 %collective-permute-start = (bf16[8,1024]{1,0:T(8,128)(2,1)S(1)}, bf16[8,1024]{1,0:T(8,128)(2,1)S(1)}, u32[]{:S(2)}, u32[]{:S(2)}) collective-permute-start(bf16[8,1024]{1,0:T(8,128)(2,1)S(1)} %fusion.27), channel_id=1, source_target_pairs={{0,2},{2,4},{4,6},{6,8},{8,10},{10,12},{12,14},{14,16},{16,18},{18... | collective-permute-start | bytes 49160 | tf_op jit(solution)/shard_map/ppermute | solution.py:17
  66.2 44.6 %collective-permute-start.3 = (bf16[8,1024]{1,0:T(8,128)(2,1)S(1)}, bf16[8,1024]{1,0:T(8,128)(2,1)S(1)}, u32[]{:S(2)}, u32[]{:S(2)}) collective-permute-start(bf16[8,1024]{1,0:T(8,128)(2,1)S(1)} %get-tuple-element.3), channel_id=1, source_target_pairs={{2,0},{4,2},{6,4},{8,6},{10,8},{12,10},{14,12},{16,14},{18,16},{20... | collective-permute-start | bytes 49160 | tf_op jit(solution)/shard_map/ppermute | solution.py:18
  67.5 45.5 %collective-permute-start.2 = (bf16[8,1024]{1,0:T(8,128)(2,1)S(1)}, bf16[8,1024]{1,0:T(8,128)(2,1)S(1)}, u32[]{:S(2)}, u32[]{:S(2)}) collective-permute-start(bf16[8,1024]{1,0:T(8,128)(2,1)S(1)} %get-tuple-element.3), channel_id=1, source_target_pairs={{0,2},{2,4},{4,6},{6,8},{8,10},{10,12},{12,14},{14,16},{16,18},{18... | collective-permute-start | bytes 49160 | tf_op jit(solution)/shard_map/ppermute | solution.py:17
Sparse Core Ops, SparseCore 0:
  9.6 19.4 all-gather.3
where the time goes:
time: 123 us
  blocking collectives  75.5 us (61%)
  matrix products  18 us (15%)
  between operations  14.8 us (12%)
  starting transfers between devices  12.7 us (10%)
    all_gather x2, blocking collectives, far_field(): lax.all_gather(coef, 'cluster', axis=1, tiled=True)  75.5 us
    dot_general x6, matrix products, near_field(): lax.dot_general(columns, near_blocks[k], (((1,), (1,)), ((), ())), prefer...  14.8 us
    ppermute x2, starting transfers between devices, with_halo(): before = lax.ppermute(last, axis, up)  10 us
    ppermute x2, starting transfers between devices, with_halo(): after = lax.ppermute(initial, axis, down)  2.59 us
  transfers between devices with their start and end apart: 5, of which 0 were waited for; matrix products, arithmetic and copies ran while one was open for 11% of the time, Pallas kernels for 0%

commit v1 on v0

v1 whole, which is shorter than its diff:
```python
import functools

import jax
import jax.numpy as jnp
from jax import lax
from jax.experimental import pallas as pl
from jax.experimental.pallas import tpu as pltpu
from jax.sharding import PartitionSpec as P

step_length = 0.5
damping = 0.5

MESH = pl.DeviceIdType.MESH
ROWS = (((1,), (1,)), ((), ()))


def split(value):
    high = value.astype(jnp.bfloat16)
    low = (value - high.astype(jnp.float32)).astype(jnp.bfloat16)
    return high, low


def kernel(
    n,
    log_rate_hbm,
    state_hbm,
    rate_coef_hbm,
    state_coef_hbm,
    near_hbm,
    basis_hbm,
    coupling_hbm,
    factors_hbm,
    ranks_ref,
    log_rate_out,
    state_out,
    log_rate_ref,
    state_ref,
    rate_coef_ref,
    state_coef_ref,
    near_ref,
    basis_ref,
    coupling_ref,
    factors_ref,
    far_in,
    far_out,
    halves,
    halo,
    coef_send,
    coef_recv,
    part_send,
    part_recv,
    load_sem,
    halo_send_sem,
    halo_recv_sem,
    coef_send_sem,
    coef_recv_sem,
    part_send_sem,
    part_recv_sem,
):
    me = lax.axis_index("cluster")
    core = lax.axis_index("ens")
    other = 1 - core
    members, rows = log_rate_ref.shape
    half = rows // 2
    widest = basis_ref.shape[0]

    loads = [
        pltpu.make_async_copy(source, target, load_sem.at[i])
        for i, (source, target) in enumerate(
            (
                (log_rate_hbm, log_rate_ref),
                (basis_hbm, basis_ref),
                (state_hbm, state_ref),
                (coupling_hbm, coupling_ref),
                (factors_hbm, factors_ref),
                (near_hbm, near_ref),
                (rate_coef_hbm, rate_coef_ref),
                (state_coef_hbm, state_coef_ref),
            )
        )
    ]
    for load in loads:
        load.start()

    barrier = pltpu.get_barrier_semaphore()

    def greet(cluster, ens):
        pl.semaphore_signal(barrier, inc=1, device_id=(cluster, ens), device_id_type=MESH)

    for d in range(1, n):
        greet(lax.rem(me + d, n), core)
    greet(me, other)

    @pl.when(me > 0)
    def _():
        greet(me - 1, other)

    @pl.when(me < n - 1)
    def _():
        greet(me + 1, other)

    own_rank = ranks_ref[0]
    lane = lax.broadcasted_iota(jnp.int32, (members, 2 * widest), 1)
    lane_rank = lax.rem(lane, widest)

    zero_coef = jnp.zeros((members, 2 * widest), coef_recv.dtype)
    zero_half = jnp.zeros((members, half), halo.dtype)
    for section in range(2):
        coef_recv[section, me] = zero_coef

        @pl.when(me > 0)
        def _():
            coef_recv[section, jnp.maximum(me - 1, 0)] = zero_coef

        @pl.when(me < n - 1)
        def _():
            coef_recv[section, jnp.minimum(me + 1, n - 1)] = zero_coef

        @pl.when(me == 0)
        def _():
            for slot in range(2):
                halo[section, 0, slot] = zero_half

        @pl.when(me == n - 1)
        def _():
            for slot in range(2):
                halo[section, 2, slot] = zero_half

    def halo_copy(section, k, slot, cluster):
        ens = core if slot == 0 else other
        return pltpu.make_async_remote_copy(
            src_ref=halves.at[section, ens],
            dst_ref=halo.at[section, k, slot],
            send_sem=halo_send_sem.at[section, k, slot],
            recv_sem=halo_recv_sem.at[section, k, slot],
            device_id=(cluster, ens),
            device_id_type=MESH,
        )

    def coef_copy(section, cluster):
        return pltpu.make_async_remote_copy(
            src_ref=coef_send.at[section],
            dst_ref=coef_recv.at[section, me],
            send_sem=coef_send_sem.at[section, cluster],
            recv_sem=coef_recv_sem.at[section, me],
            device_id=(cluster, core),
            device_id_type=MESH,
        )

    def coef_arrival(section, cluster):
        return pltpu.make_async_remote_copy(
            src_ref=coef_send.at[section],
            dst_ref=coef_recv.at[section, cluster],
            send_sem=coef_send_sem.at[section, cluster],
            recv_sem=coef_recv_sem.at[section, cluster],
            device_id=(cluster, core),
            device_id_type=MESH,
        )

    def part_copy(section):
        return pltpu.make_async_remote_copy(
            src_ref=part_send.at[section],
            dst_ref=part_recv.at[section],
            send_sem=part_send_sem.at[section],
            recv_sem=part_recv_sem.at[section],
            device_id=(me, other),
            device_id_type=MESH,
        )

    def each_far(action):
        for d in range(2, n - 1):
            action(lax.rem(me + d, n))

        @pl.when(me == 0)
        def _():
            action(jnp.int32(n - 1))

        @pl.when(me == n - 1)
        def _():
            action(jnp.int32(0))

    def prepare():
        loads[3].wait()
        row = lax.broadcasted_iota(jnp.int32, (widest, 2 * widest), 0)
        kept = row < own_rank
        for j in range(n):
            block = coupling_ref[:, j * widest : (j + 1) * widest]
            block = jnp.concatenate([block, block], axis=1)
            block = jnp.where(jnp.logical_and(kept, jnp.abs(me - j) > 1), block, 0.0)
            high, low = split(block)
            far_in[0:widest, 2 * j * widest : 2 * (j + 1) * widest] = high
            far_in[widest : 2 * widest, 2 * j * widest : 2 * (j + 1) * widest] = low
        loads[4].wait()
        high, low = split(factors_ref[...])
        far_out[0:widest] = high
        far_out[widest : 2 * widest] = high
        far_out[2 * widest : 3 * widest] = low
        far_out[3 * widest : 4 * widest] = low

    def rates(section, current_logarithm):
        rate = jnp.exp(current_logarithm)
        deficit = (rate - 1.0).astype(jnp.bfloat16)
        halves[section, 0] = deficit[:, :half]
        halves[section, 1] = deficit[:, half:]
        halo[section, 1, 0] = halves[section, core]
        basis = basis_ref[...]
        coef = lax.dot_general(
            deficit,
            jnp.concatenate([basis, basis], axis=0),
            ROWS,
            preferred_element_type=jnp.float32,
        )
        coef = jnp.where(lane_rank < own_rank, coef, 0.0)
        high = coef.astype(jnp.bfloat16).astype(jnp.float32)
        coef_send[section] = jnp.where(lane < widest, high, coef - high).astype(jnp.bfloat16)

        if section == 0:
            greeted = n + jnp.where(me > 0, 1, 0) + jnp.where(me < n - 1, 1, 0)
            pl.semaphore_wait(barrier, greeted)

        each_far(lambda cluster: coef_copy(section, cluster).start())

        @pl.when(me > 0)
        def _():
            for slot in range(2):
                halo_copy(section, 2, slot, me - 1).start()

        @pl.when(me < n - 1)
        def _():
            for slot in range(2):
                halo_copy(section, 0, slot, me + 1).start()

        halo_copy(section, 1, 1, me).start()

        if section == 0:
            prepare()
            loads[5].wait()

        def near(k):
            columns = jnp.concatenate([halo[section, k, 0], halo[section, k, 1]], axis=0)
            return lax.dot_general(
                columns, near_ref[k], ROWS, preferred_element_type=jnp.float32
            )

        halo_copy(section, 1, 1, me).wait_recv()
        total = near(1)

        @pl.when(me > 0)
        def _():
            for slot in range(2):
                halo_copy(section, 0, slot, me - 1).wait_recv()

        total = total + near(0)

        @pl.when(me < n - 1)
        def _():
            for slot in range(2):
                halo_copy(section, 2, slot, me + 1).wait_recv()

        total = total + near(2)
        part_send[section] = total[members:]
        part_copy(section).start()

        each_far(lambda cluster: coef_arrival(section, cluster).wait_recv())
        coefs = jnp.concatenate([coef_recv[section, j] for j in range(n)], axis=1)
        reduced = lax.dot_general(coefs, far_in[...], ROWS, preferred_element_type=jnp.float32)
        high, low = split(reduced)
        reduced = jnp.concatenate(
            [jnp.concatenate([high, high], axis=1), jnp.concatenate([low, low], axis=1)], axis=0
        )
        far = jnp.dot(reduced, far_out[...], preferred_element_type=jnp.float32)
        stress_rate = total[:members] + (far[:members] + far[members:])
        part_copy(section).wait_recv()
        return rate, stress_rate + part_recv[section]

    loads[0].wait()
    loads[1].wait()
    log_rate = log_rate_ref[...]
    rate, stress_one = rates(0, log_rate)
    loads[2].wait()
    loads[6].wait()
    loads[7].wait()
    state = state_ref[...]
    rate_coef = rate_coef_ref[...]
    state_coef = state_coef_ref[...]
    state_one = jnp.exp(-state) - rate
    rate_one = (stress_one - state_coef * state_one) / (rate_coef + damping * rate)
    second, stress_two = rates(1, log_rate + step_length * rate_one)
    state_two = jnp.exp(-(state + step_length * state_one)) - second
    rate_two = (stress_two - state_coef * state_two) / (rate_coef + damping * second)
    log_rate_out[...] = log_rate + 0.5 * step_length * (rate_one + rate_two)
    state_out[...] = state + 0.5 * step_length * (state_one + state_two)

    for section in range(2):
        each_far(lambda cluster: coef_copy(section, cluster).wait_send())

        @pl.when(me > 0)
        def _():
            for slot in range(2):
                halo_copy(section, 2, slot, me - 1).wait_send()

        @pl.when(me < n - 1)
        def _():
            for slot in range(2):
                halo_copy(section, 0, slot, me + 1).wait_send()

        halo_copy(section, 1, 1, me).wait_send()
        part_copy(section).wait_send()


def local(n, *args):
    log_rate, near_weight, col_basis, coupling, factors = (args[i] for i in (0, 4, 5, 6, 7))
    members, rows = log_rate.shape
    half = near_weight.shape[2]
    widest = col_basis.shape[0]
    f32, bf16 = jnp.float32, jnp.bfloat16
    anywhere = pl.BlockSpec(memory_space=pl.ANY)
    vmem = pl.BlockSpec(memory_space=pltpu.VMEM)
    return tuple(
        pl.pallas_call(
            functools.partial(kernel, n),
            out_shape=[jax.ShapeDtypeStruct((members, rows), f32)] * 2,
            in_specs=[anywhere] * 8 + [pl.BlockSpec(memory_space=pltpu.SMEM)],
            out_specs=[vmem] * 2,
            scratch_shapes=[
                pltpu.VMEM((members, rows), f32),
                pltpu.VMEM((members, rows), f32),
                pltpu.VMEM((members, rows), f32),
                pltpu.VMEM((members, rows), f32),
                pltpu.VMEM(near_weight.shape, bf16),
                pltpu.VMEM(col_basis.shape, bf16),
                pltpu.VMEM(coupling.shape, f32),
                pltpu.VMEM(factors.shape, f32),
                pltpu.VMEM((2 * widest, n * 2 * widest), bf16),
                pltpu.VMEM((4 * widest, rows), bf16),
                pltpu.VMEM((2, 2, members, half), bf16),
                pltpu.VMEM((2, 3, 2, members, half), bf16),
                pltpu.VMEM((2, members, 2 * widest), bf16),
                pltpu.VMEM((2, n, members, 2 * widest), bf16),
                pltpu.VMEM((2, members, rows), f32),
                pltpu.VMEM((2, members, rows), f32),
                pltpu.SemaphoreType.DMA((8,)),
                pltpu.SemaphoreType.DMA((2, 3, 2)),
                pltpu.SemaphoreType.DMA((2, 3, 2)),
                pltpu.SemaphoreType.DMA((2, n)),
                pltpu.SemaphoreType.DMA((2, n)),
                pltpu.SemaphoreType.DMA((2,)),
                pltpu.SemaphoreType.DMA((2,)),
            ],
            compiler_params=pltpu.CompilerParams(
                collective_id=0, has_side_effects=True, vmem_limit_bytes=60 * 1024 * 1024
            ),
        )(*args)
    )


def solution(mesh):
    in_specs = (
        P("ens", "cluster"),
        P("ens", "cluster"),
        P("ens", "cluster"),
        P("ens", "cluster"),
        P(None, "cluster", "ens"),
        P(None, "cluster"),
        P("cluster", None),
        P(None, "cluster"),
        P("cluster"),
    )
    out_specs = (P("ens", "cluster"), P("ens", "cluster"))
    return jax.shard_map(
        functools.partial(local, mesh.shape["cluster"]),
        mesh=mesh,
        in_specs=in_specs,
        out_specs=out_specs,
        check_vma=False,
    )
```

time: 123 us -> 23.6 us (0.19)
  blocking collectives: 75.5 us -> 0 us
  Pallas kernels: 0 us -> 19.3 us
  matrix products: 18 us -> 0 us
  between operations: 14.8 us -> 1.29 us
  starting transfers between devices: 12.7 us -> 0 us
  local copies, waits for them, and re-layouts: 0.24 us -> 2.75 us
    all_gather x2 -> x0, blocking collectives: 75.5 us -> none  [far_field(): lax.all_gather(coef, 'cluster', axis=1, tiled=True)]
    pallas_call x0 -> x1, Pallas kernels: none -> 19.3 us  [local(): pl.pallas_call(functools.partial(kernel, n), out_shape=[jax.ShapeDtypeStr...]
    dot_general x12 -> x0, matrix products: 18 us -> none  [the longest x6 14.8 us: near_field(): lax.dot_general(columns, near_blocks[k], (((1,), (1,)), ((), ())), prefer...]
    ppermute x4 -> x0, starting transfers between devices: 12.6 us -> none  [the longest x2 10 us: with_halo(): before = lax.ppermute(last, axis, up)]
    unnamed x16 -> x2, local copies, waits for them, and re-layouts: 0.22 us -> 2.75 us
  transfers between devices with their start and end apart: 5 -> 0, of which waited for: 0 -> 0; matrix products, arithmetic and copies ran while one was open for 11% -> 0% of each run, Pallas kernels for 0% -> 0%
where the time goes in v1:
time: 23.6 us; the launch traced here: 23.3 us
  Pallas kernels  19.3 us (82%)
  local copies, waits for them, and re-layouts  2.75 us (12%)
  between operations  1.29 us (5%)
    pallas_call x1, Pallas kernels, local(): pl.pallas_call(functools.partial(kernel, n), out_shape=[jax.ShapeDtypeStr...  19.3 us
    unnamed x2, local copies, waits for them, and re-layouts  2.75 us

profile of v1, /device:TPU:0, one launch (start us, length us, event | category | flops | bytes accessed | tf_op | source)
XLA Modules:
  0.0 23.3 jit_solution(2147035478953543637)
XLA Ops:
  1.3 19.3 %shard_map.104 = (f32[8,1024]{1,0:T(8,128)}, f32[8,1024]{1,0:T(8,128)}) custom-call(f32[8,1024]{1,0:T(8,128)} %log_rate_hbm.1, f32[8,1024]{1,0:T(8,128)} %state_hbm.1, f32[8,1024]{1,0:T(8,128)} %rate_coef_hbm.1, f32[8,1024]{1,0:T(8,128)} %state_coef_hbm.1, bf16[3,1024,512]{2,1,0:T(8,128)(2,1)} %near_hbm.1, bf16[64,1024]{1,0:T(8,128)(2,1)} %basis_hbm.1, ...), custom_call_target="tpu_custom_call" | custom-call | tf_op jit(solution)/shard_map/pallas_call | solution.py:320
  20.6 1.4 %copy.14 = f32[8,1024]{1,0:T(8,128)} copy(f32[8,1024]{1,0:T(8,128)} %get-tuple-element.4) | data formatting | bytes 65536
  21.9 1.4 %copy.15 = f32[8,1024]{1,0:T(8,128)} copy(f32[8,1024]{1,0:T(8,128)} %get-tuple-element.5) | data formatting | bytes 65536

commit v2 on v1

--- a/solution.py
+++ b/solution.py
@@ -30,9 +30,9 @@
     basis_hbm,
     coupling_hbm,
     factors_hbm,
+    ranks_hbm,
+    sums_out,
     ranks_ref,
-    log_rate_out,
-    state_out,
     log_rate_ref,
     state_ref,
     rate_coef_ref,
@@ -76,11 +76,12 @@
                 (near_hbm, near_ref),
                 (rate_coef_hbm, rate_coef_ref),
                 (state_coef_hbm, state_coef_ref),
+                (ranks_hbm, ranks_ref),
             )
         )
     ]
-    for load in loads:
-        load.start()
+    for i in (0, 1, 8, 2, 3, 4, 5, 6, 7):
+        loads[i].start()
 
     barrier = pltpu.get_barrier_semaphore()
 
@@ -99,7 +100,6 @@
     def _():
         greet(me + 1, other)
 
-    own_rank = ranks_ref[0]
     lane = lax.broadcasted_iota(jnp.int32, (members, 2 * widest), 1)
     lane_rank = lax.rem(lane, widest)
 
@@ -168,7 +168,7 @@
         )
 
     def each_far(action):
-        for d in range(2, n - 1):
+        for d in sorted(range(2, n - 1), key=lambda d: abs(2 * d - n)):
             action(lax.rem(me + d, n))
 
         @pl.when(me == 0)
@@ -179,7 +179,7 @@
         def _():
             action(jnp.int32(0))
 
-    def prepare():
+    def prepare(own_rank):
         loads[3].wait()
         row = lax.broadcasted_iota(jnp.int32, (widest, 2 * widest), 0)
         kept = row < own_rank
@@ -197,7 +197,7 @@
         far_out[2 * widest : 3 * widest] = low
         far_out[3 * widest : 4 * widest] = low
 
-    def rates(section, current_logarithm):
+    def rates(section, current_logarithm, own_rank):
         rate = jnp.exp(current_logarithm)
         deficit = (rate - 1.0).astype(jnp.bfloat16)
         halves[section, 0] = deficit[:, :half]
@@ -233,7 +233,7 @@
         halo_copy(section, 1, 1, me).start()
 
         if section == 0:
-            prepare()
+            prepare(own_rank)
             loads[5].wait()
 
         def near(k):
@@ -275,8 +275,10 @@
 
     loads[0].wait()
     loads[1].wait()
+    loads[8].wait()
+    own_rank = ranks_ref[0]
     log_rate = log_rate_ref[...]
-    rate, stress_one = rates(0, log_rate)
+    rate, stress_one = rates(0, log_rate, own_rank)
     loads[2].wait()
     loads[6].wait()
     loads[7].wait()
@@ -285,11 +287,11 @@
     state_coef = state_coef_ref[...]
     state_one = jnp.exp(-state) - rate
     rate_one = (stress_one - state_coef * state_one) / (rate_coef + damping * rate)
-    second, stress_two = rates(1, log_rate + step_length * rate_one)
+    second, stress_two = rates(1, log_rate + step_length * rate_one, own_rank)
     state_two = jnp.exp(-(state + step_length * state_one)) - second
     rate_two = (stress_two - state_coef * state_two) / (rate_coef + damping * second)
-    log_rate_out[...] = log_rate + 0.5 * step_length * (rate_one + rate_two)
-    state_out[...] = state + 0.5 * step_length * (state_one + state_two)
+    sums_out[0] = rate_one + rate_two
+    sums_out[1] = state_one + state_two
 
     for section in range(2):
         each_far(lambda cluster: coef_copy(section, cluster).wait_send())
@@ -306,6 +308,11 @@
 
         halo_copy(section, 1, 1, me).wait_send()
         part_copy(section).wait_send()
+
+
+def finish(sums_ref, log_rate_ref, state_ref, log_rate_out, state_out):
+    log_rate_out[...] = log_rate_ref[...] + 0.5 * step_length * sums_ref[0]
+    state_out[...] = state_ref[...] + 0.5 * step_length * sums_ref[1]
 
 
 def local(n, *args):
@@ -314,15 +321,15 @@
     half = near_weight.shape[2]
     widest = col_basis.shape[0]
     f32, bf16 = jnp.float32, jnp.bfloat16
-    anywhere = pl.BlockSpec(memory_space=pl.ANY)
+    in_hbm = pl.BlockSpec(memory_space=pltpu.HBM)
     vmem = pl.BlockSpec(memory_space=pltpu.VMEM)
-    return tuple(
-        pl.pallas_call(
+    sums = pl.pallas_call(
             functools.partial(kernel, n),
-            out_shape=[jax.ShapeDtypeStruct((members, rows), f32)] * 2,
-            in_specs=[anywhere] * 8 + [pl.BlockSpec(memory_space=pltpu.SMEM)],
-            out_specs=[vmem] * 2,
+            out_shape=pltpu.VMEM((2, members, rows), f32),
+            in_specs=[in_hbm] * 9,
+            out_specs=vmem,
             scratch_shapes=[
+                pltpu.SMEM((1,), jnp.int32),
                 pltpu.VMEM((members, rows), f32),
                 pltpu.VMEM((members, rows), f32),
                 pltpu.VMEM((members, rows), f32),
@@ -339,7 +346,7 @@
                 pltpu.VMEM((2, n, members, 2 * widest), bf16),
                 pltpu.VMEM((2, members, rows), f32),
                 pltpu.VMEM((2, members, rows), f32),
-                pltpu.SemaphoreType.DMA((8,)),
+                pltpu.SemaphoreType.DMA((9,)),
                 pltpu.SemaphoreType.DMA((2, 3, 2)),
                 pltpu.SemaphoreType.DMA((2, 3, 2)),
                 pltpu.SemaphoreType.DMA((2, n)),
@@ -351,6 +358,14 @@
                 collective_id=0, has_side_effects=True, vmem_limit_bytes=60 * 1024 * 1024
             ),
         )(*args)
+    return tuple(
+        pl.pallas_call(
+            finish,
+            out_shape=[jax.ShapeDtypeStruct((members, rows), f32)] * 2,
+            in_specs=[vmem] * 3,
+            out_specs=[vmem] * 2,
+            compiler_params=pltpu.CompilerParams(vmem_limit_bytes=1024 * 1024),
+        )(sums, args[0], args[1])
     )
 
 

time: 23.6 us -> 20.8 us (0.88)
  local copies, waits for them, and re-layouts: 2.75 us -> 0.01 us
    unnamed x2 -> x4, local copies, waits for them, and re-layouts: 2.75 us -> 0.01 us
    pallas_call x1 -> x2, Pallas kernels: 19.3 us -> 19.3 us  [the longest x1 18.7 us: local(): pl.pallas_call(functools.partial(kernel, n), out_shape=pltpu.VMEM((2, mem...]
where the time goes in v2:
time: 20.8 us; the launch traced here: 20.6 us
  Pallas kernels  19.3 us (93%)
  between operations  1.33 us (6%)
    pallas_call x1, Pallas kernels, local(): pl.pallas_call(functools.partial(kernel, n), out_shape=pltpu.VMEM((2, mem...  18.7 us
    pallas_call x1, Pallas kernels, local(): pl.pallas_call(finish, out_shape=[jax.ShapeDtypeStruct((members, rows), f...  0.63 us

profile of v2, /device:TPU:0, one launch (start us, length us, event | category | flops | bytes accessed | tf_op | source)
XLA Modules:
  0.0 20.6 jit_solution(4221563532954556434)
XLA Ops:
  0.6 0.0 copy-start.1
  0.6 0.0 copy-start
  1.3 18.7 %shard_map.104.sums_ref = f32[2,8,1024]{2,1,0:T(8,128)S(1)} custom-call(f32[8,1024]{1,0:T(8,128)} %log_rate_ref.1, f32[8,1024]{1,0:T(8,128)} %state_ref.1, f32[8,1024]{1,0:T(8,128)} %rate_coef_hbm.1, f32[8,1024]{1,0:T(8,128)} %state_coef_hbm.1, bf16[3,1024,512]{2,1,0:T(8,128)(2,1)} %near_hbm.1, bf16[64,1024]{1,0:T(8,128)(2,1)} %basis_hbm.1, ...), custom_call_target="tpu_custom_call" | custom-call | tf_op jit(solution)/shard_map/pallas_call | solution.py:326
  20.0 0.0 copy-done.1
  20.0 0.0 copy-done
  20.0 0.6 %shard_map.105 = (f32[8,1024]{1,0:T(8,128)}, f32[8,1024]{1,0:T(8,128)}) custom-call(f32[2,8,1024]{2,1,0:T(8,128)S(1)} %shard_map.104.sums_ref, f32[8,1024]{1,0:T(8,128)S(1)} %copy-done, f32[8,1024]{1,0:T(8,128)S(1)} %copy-done.1), custom_call_target="tpu_custom_call" | custom-call | tf_op jit(solution)/shard_map/pallas_call | solution.py:362
Async XLA Ops:
  0.6 19.4 %copy-start.1 = (f32[8,1024]{1,0:T(8,128)S(1)}, f32[8,1024]{1,0:T(8,128)}, u32[]{:S(2)}) copy-start(f32[8,1024]{1,0:T(8,128)} %state_ref.1) | copy-start | bytes 98308
  0.6 19.4 %copy-start = (f32[8,1024]{1,0:T(8,128)S(1)}, f32[8,1024]{1,0:T(8,128)}, u32[]{:S(2)}) copy-start(f32[8,1024]{1,0:T(8,128)} %log_rate_ref.1) | copy-start | bytes 98308

commit v3 on v2

--- a/solution.py
+++ b/solution.py
@@ -54,6 +54,7 @@
     halo_recv_sem,
     coef_send_sem,
     coef_recv_sem,
+    relay_send_sem,
     part_send_sem,
     part_recv_sem,
 ):
@@ -88,17 +89,48 @@
     def greet(cluster, ens):
         pl.semaphore_signal(barrier, inc=1, device_id=(cluster, ens), device_id_type=MESH)
 
-    for d in range(1, n):
-        greet(lax.rem(me + d, n), core)
+    plane = 4 if n % 4 == 0 and n > 4 else n
+    planes = n // plane
+    place, level = lax.rem(me, plane), lax.div(me, plane)
+
+    def at(turn, up):
+        if plane == n:
+            return lax.rem(me + turn, n)
+        places = (
+            place,
+            place + 1 - 2 * lax.rem(place, 2),
+            place + 2 - 4 * lax.div(place, 2),
+            3 - place,
+        )
+        return lax.rem(level + up, planes) * plane + places[turn]
+
+    beside = {1, planes - 1}
+    inner = sorted(range(1, plane), reverse=True)
+    direct = [(turn, 0) for turn in inner]
+    relays = []
+    if planes > 1:
+        ups = sorted(range(1, planes), key=lambda up: abs(2 * up - planes))
+        direct += [(0, up) for up in ups]
+        direct += [(turn, up) for turn in (1, 2) for up in ups if up in beside]
+        relays = [(3, up) for up in ups]
+        relays += [(turn, up) for turn in (1, 2) for up in ups if up not in beside]
+
+    for turn, up in direct:
+        greet(at(turn, up), core)
     greet(me, other)
-
-    @pl.when(me > 0)
-    def _():
-        greet(me - 1, other)
-
-    @pl.when(me < n - 1)
-    def _():
-        greet(me + 1, other)
+    greeted = len(direct) + 1
+
+    starts = jnp.logical_and(me > 0, place == 0)
+    ends = jnp.logical_and(me < n - 1, place == plane - 1)
+    pairs = ((me > 0, me - 1, other), (me < n - 1, me + 1, other))
+    if planes > 1:
+        pairs += ((starts, me - 1, core), (ends, me + 1, core))
+    for there, cluster, ens in pairs:
+        greeted = greeted + jnp.where(there, 1, 0)
+
+        @pl.when(there)
+        def _():
+            greet(cluster, ens)
 
     lane = lax.broadcasted_iota(jnp.int32, (members, 2 * widest), 1)
     lane_rank = lax.rem(lane, widest)
@@ -107,14 +139,15 @@
     zero_half = jnp.zeros((members, half), halo.dtype)
     for section in range(2):
         coef_recv[section, me] = zero_coef
-
-        @pl.when(me > 0)
-        def _():
-            coef_recv[section, jnp.maximum(me - 1, 0)] = zero_coef
-
-        @pl.when(me < n - 1)
-        def _():
-            coef_recv[section, jnp.minimum(me + 1, n - 1)] = zero_coef
+        if section == 1:
+
+            @pl.when(me > 0)
+            def _():
+                coef_recv[section, jnp.maximum(me - 1, 0)] = zero_coef
+
+            @pl.when(me < n - 1)
+            def _():
+                coef_recv[section, jnp.minimum(me + 1, n - 1)] = zero_coef
 
         @pl.when(me == 0)
         def _():
@@ -156,6 +189,22 @@
             device_id=(cluster, core),
             device_id_type=MESH,
         )
+
+    def relay_copy(at_relay):
+        turn, up = relays[at_relay]
+        source = at(turn, 0)
+        return pltpu.make_async_remote_copy(
+            src_ref=coef_recv.at[0, source],
+            dst_ref=coef_recv.at[0, source],
+            send_sem=relay_send_sem.at[at_relay],
+            recv_sem=coef_recv_sem.at[0, source],
+            device_id=(at(0, up), core),
+            device_id_type=MESH,
+        )
+
+    def each_direct(action):
+        for turn, up in direct:
+            action(at(turn, up))
 
     def part_copy(section):
         return pltpu.make_async_remote_copy(
@@ -215,10 +264,10 @@
         coef_send[section] = jnp.where(lane < widest, high, coef - high).astype(jnp.bfloat16)
 
         if section == 0:
-            greeted = n + jnp.where(me > 0, 1, 0) + jnp.where(me < n - 1, 1, 0)
             pl.semaphore_wait(barrier, greeted)
-
-        each_far(lambda cluster: coef_copy(section, cluster).start())
+            each_direct(lambda cluster: coef_copy(section, cluster).start())
+        else:
+            each_far(lambda cluster: coef_copy(section, cluster).start())
 
         @pl.when(me > 0)
         def _():
@@ -245,6 +294,13 @@
         halo_copy(section, 1, 1, me).wait_recv()
         total = near(1)
 
+        if section == 0:
+            for turn in inner:
+                coef_arrival(section, at(turn, 0)).wait_recv()
+                for i, (relayed, _) in enumerate(relays):
+                    if relayed == turn:
+                        relay_copy(i).start()
+
         @pl.when(me > 0)
         def _():
             for slot in range(2):
@@ -261,7 +317,12 @@
         part_send[section] = total[members:]
         part_copy(section).start()
 
-        each_far(lambda cluster: coef_arrival(section, cluster).wait_recv())
+        if section == 0:
+            for turn in range(min(plane, 4) if planes > 1 else 0):
+                for up in range(1, planes):
+                    coef_arrival(section, at(turn, up)).wait_recv()
+        else:
+            each_far(lambda cluster: coef_arrival(section, cluster).wait_recv())
         coefs = jnp.concatenate([coef_recv[section, j] for j in range(n)], axis=1)
         reduced = lax.dot_general(coefs, far_in[...], ROWS, preferred_element_type=jnp.float32)
         high, low = split(reduced)
@@ -294,7 +355,12 @@
     sums_out[1] = state_one + state_two
 
     for section in range(2):
-        each_far(lambda cluster: coef_copy(section, cluster).wait_send())
+        if section == 0:
+            each_direct(lambda cluster: coef_copy(section, cluster).wait_send())
+            for i in range(len(relays)):
+                relay_copy(i).wait_send()
+        else:
+            each_far(lambda cluster: coef_copy(section, cluster).wait_send())
 
         @pl.when(me > 0)
         def _():
@@ -351,6 +417,7 @@
                 pltpu.SemaphoreType.DMA((2, 3, 2)),
                 pltpu.SemaphoreType.DMA((2, n)),
                 pltpu.SemaphoreType.DMA((2, n)),
+                pltpu.SemaphoreType.DMA((n,)),
                 pltpu.SemaphoreType.DMA((2,)),
                 pltpu.SemaphoreType.DMA((2,)),
             ],

time: 20.8 us -> 22 us (1.058)
  Pallas kernels: 19.3 us -> 20.5 us
    pallas_call x1, Pallas kernels: 18.7 us -> 19.9 us  [local(): pl.pallas_call(functools.partial(kernel, n), out_shape=pltpu.VMEM((2, mem...]
where the time goes in v3:
time: 22 us; the launch traced here: 21.9 us
  Pallas kernels  20.5 us (93%)
  between operations  1.33 us (6%)
    pallas_call x1, Pallas kernels, local(): pl.pallas_call(functools.partial(kernel, n), out_shape=pltpu.VMEM((2, mem...  19.9 us
    pallas_call x1, Pallas kernels, local(): pl.pallas_call(finish, out_shape=[jax.ShapeDtypeStruct((members, rows), f...  0.63 us

profile of v3, /device:TPU:0, one launch (start us, length us, event | category | flops | bytes accessed | tf_op | source)
XLA Modules:
  0.0 21.9 jit_solution(13103361128667708320)
XLA Ops:
  0.6 0.0 copy-start.1
  0.6 0.0 copy-start
  1.3 19.9 %shard_map.104.sums_ref = f32[2,8,1024]{2,1,0:T(8,128)S(1)} custom-call(f32[8,1024]{1,0:T(8,128)} %log_rate_ref.1, f32[8,1024]{1,0:T(8,128)} %state_ref.1, f32[8,1024]{1,0:T(8,128)} %rate_coef_hbm.1, f32[8,1024]{1,0:T(8,128)} %state_coef_hbm.1, bf16[3,1024,512]{2,1,0:T(8,128)(2,1)} %near_hbm.1, bf16[64,1024]{1,0:T(8,128)(2,1)} %basis_hbm.1, ...), custom_call_target="tpu_custom_call" | custom-call | tf_op jit(solution)/shard_map/pallas_call | solution.py:392
  21.2 0.0 copy-done.1
  21.2 0.0 copy-done
  21.2 0.6 %shard_map.105 = (f32[8,1024]{1,0:T(8,128)}, f32[8,1024]{1,0:T(8,128)}) custom-call(f32[2,8,1024]{2,1,0:T(8,128)S(1)} %shard_map.104.sums_ref, f32[8,1024]{1,0:T(8,128)S(1)} %copy-done, f32[8,1024]{1,0:T(8,128)S(1)} %copy-done.1), custom_call_target="tpu_custom_call" | custom-call | tf_op jit(solution)/shard_map/pallas_call | solution.py:429
Async XLA Ops:
  0.6 20.6 %copy-start.1 = (f32[8,1024]{1,0:T(8,128)S(1)}, f32[8,1024]{1,0:T(8,128)}, u32[]{:S(2)}) copy-start(f32[8,1024]{1,0:T(8,128)} %state_ref.1) | copy-start | bytes 98308
  0.6 20.6 %copy-start = (f32[8,1024]{1,0:T(8,128)S(1)}, f32[8,1024]{1,0:T(8,128)}, u32[]{:S(2)}) copy-start(f32[8,1024]{1,0:T(8,128)} %log_rate_ref.1) | copy-start | bytes 98308
